TPU v7x, 32 devices: a whole 2x2x4 slice. The times are simulated.
32 devices in a mesh: row: 4 (over y, core), col: 8 (over z, x).
Axes of the slice: x: 2, y: 2, z: 4, core: 2. Of those that a mesh axis runs over, the one named last changes fastest.
Arguments:
- support_views: float32 [256, 4, 3, 1024], P(('row', 'col')), may hold values from -6 to 6
- support_pick: int32 [256], P(('row', 'col')), may hold values from 0 to 3
- target_views: float32 [256, 4, 3, 1024], P(('row', 'col')), may hold values from -6 to 6
- target_pick: int32 [256], P(('row', 'col')), may hold values from 0 to 3
- support_labels: float32 [256, 10], P(('row', 'col')), may hold values from -6 to 6
- target_labels: int32 [256], replicated, may hold values from 0 to 9
Outputs:
- support_grad: float32 [256, 3, 1024], P(('row', 'col'))
- label_grad: float32 [256, 10], P(('row', 'col'))
- loss: float32 [], replicated
All inputs are finite; a program needn't handle non-finite values.
Results may differ from a plain program's by a relative error of at most 0.00055.
Values sent between devices are 32-bit elements; how exact they have to be, the bound alone decides.
No kernel may reach another device: no remote copies, remote signals or barrier semaphores. Data moves between devices by JAX's collectives and lax.ppermute only.
A program may use at most 64 MiB of HBM per device.

v0:
```python
import math
import jax
import jax.numpy as jnp
from jax import lax
from jax.sharding import PartitionSpec as P

SIDE = 32
LAYERS = 3
SUPPORT = 256
bias_variance = 0.1
ridge_scale = 0.1
highest = lax.Precision.HIGHEST


def shifted(surface, offset):
    extent = surface.shape[-1]
    padding = jnp.zeros(surface.shape[:-1] + (abs(offset),), surface.dtype)
    if offset > 0:
        return jnp.concatenate([surface[..., offset:], padding], axis=-1)
    return jnp.concatenate([padding, surface[..., : extent + offset]], axis=-1)


def average(surface):
    column = jnp.arange(surface.shape[-1], dtype=jnp.int32) % SIDE
    rightward = jnp.where(column < SIDE - 1, shifted(surface, 1), 0.0)
    leftward = jnp.where(column > 0, shifted(surface, -1), 0.0)
    across = surface + leftward + rightward
    return (across + shifted(across, SIDE) + shifted(across, -SIDE)) / 9.0


def choose_view(views, picked):
    options = jnp.arange(views.shape[1], dtype=jnp.int32)
    selector = (picked[:, None] == options[None, :]).astype(jnp.float32)
    return jnp.sum(selector[:, :, None, None] * views, axis=1)


def self_maps(images):
    energy = jnp.sum(images * images, axis=1) / images.shape[1]
    current = average(energy) + bias_variance
    stacked = [current]
    for layer in range(1, LAYERS):
        current = average(current) + bias_variance
        stacked.append(current)
    return jnp.stack(stacked, axis=1)


def self_back(images, grad_maps):
    carry = grad_maps[:, -1]
    for layer in range(grad_maps.shape[1] - 2, -1, -1):
        carry = grad_maps[:, layer] + average(carry)
    return average(carry)[:, None, :] * images * (2.0 / images.shape[1])


def arc(kernel_map, first_diag, second_diag):
    scale_map = jnp.sqrt(first_diag * second_diag)
    cosine = jnp.clip(kernel_map / scale_map, -1.0, 1.0)
    sine = jnp.sqrt(1.0 - cosine * cosine)
    angle = jnp.arccos(cosine)
    value = scale_map * (sine + (jnp.pi - angle) * cosine) / jnp.pi
    slope = (jnp.pi - angle) / jnp.pi
    spread = scale_map * sine / (2.0 * jnp.pi)
    return (value, slope, spread)


def pair_forward(first, first_maps, second, second_maps):
    product = first[:, None, 0] * second[None, :, 0]
    for channel in range(1, first.shape[1]):
        product = product + first[:, None, channel] * second[None, :, channel]
    current = average(product / first.shape[1]) + bias_variance
    slopes = []
    spreads = []
    depth = first_maps.shape[1]
    for layer in range(depth):
        value, slope, spread = arc(current, first_maps[:, None, layer], second_maps[None, :, layer])
        slopes.append(slope)
        spreads.append(spread)
        if layer + 1 < depth:
            current = average(value) + bias_variance
    return (jnp.mean(value, axis=-1), slopes, spreads)


def pair_backward(first, first_maps, second, second_maps, weights, want_second):
    kernel, slopes, spreads = pair_forward(first, first_maps, second, second_maps)
    depth = first_maps.shape[1]
    grad = jnp.broadcast_to(weights[:, :, None] / first.shape[-1], slopes[0].shape)
    first_parts = []
    second_parts = []
    for layer in range(depth - 1, -1, -1):
        scaled = grad * spreads[layer]
        first_parts.insert(0, jnp.sum(scaled, axis=1) / first_maps[:, layer])
        if want_second:
            second_parts.insert(0, jnp.sum(scaled, axis=0) / second_maps[:, layer])
        grad = average(grad * slopes[layer])
    first_image = (
        jnp.stack(
            [jnp.sum(grad * second[None, :, channel], axis=1) for channel in range(first.shape[1])],
            axis=1,
        )
        / first.shape[1]
    )
    if not want_second:
        return (first_image, jnp.stack(first_parts, axis=1), None, None)
    second_image = (
        jnp.stack(
            [jnp.sum(grad * first[:, None, channel], axis=0) for channel in range(first.shape[1])],
            axis=1,
        )
        / first.shape[1]
    )
    return (
        first_image,
        jnp.stack(first_parts, axis=1),
        second_image,
        jnp.stack(second_parts, axis=1),
    )


def blocked_kernel(first, first_maps, second, second_maps):
    block_width = math.gcd(second.shape[0], 4)
    block_count = second.shape[0] // block_width

    def one_block(inputs):
        part_images, part_maps = inputs
        kernel, _, _ = pair_forward(first, first_maps, part_images, part_maps)
        return kernel

    pieces = lax.map(
        one_block,
        (
            second.reshape((block_count, block_width) + second.shape[1:]),
            second_maps.reshape((block_count, block_width) + second_maps.shape[1:]),
        ),
    )
    return jnp.transpose(pieces, (1, 0, 2)).reshape(first.shape[0], second.shape[0])


def blocked_backward(first, first_maps, second, second_maps, weights, want_second):
    block_width = math.gcd(second.shape[0], 4)
    block_count = second.shape[0] // block_width
    block_weights = jnp.transpose(
        weights.reshape(first.shape[0], block_count, block_width), (1, 0, 2)
    )

    def one_block(carry, inputs):
        part_images, part_maps, part_weights = inputs
        grad_first, maps_first, grad_second, maps_second = pair_backward(
            first, first_maps, part_images, part_maps, part_weights, want_second
        )
        return ((carry[0] + grad_first, carry[1] + maps_first), (grad_second, maps_second))

    start = (jnp.zeros(first.shape, jnp.float32), jnp.zeros(first_maps.shape, jnp.float32))
    (first_grad, first_map_grad), (second_grad, second_map_grad) = lax.scan(
        one_block,
        start,
        (
            second.reshape((block_count, block_width) + second.shape[1:]),
            second_maps.reshape((block_count, block_width) + second_maps.shape[1:]),
            block_weights,
        ),
    )
    if not want_second:
        return (first_grad, first_map_grad, None, None)
    return (
        first_grad,
        first_map_grad,
        second_grad.reshape(second.shape),
        second_map_grad.reshape(second_maps.shape),
    )


def solve_with(factor, rhs):
    halfway = lax.linalg.triangular_solve(factor, rhs, left_side=True, lower=True)
    return lax.linalg.triangular_solve(
        factor, halfway, left_side=True, lower=True, transpose_a=True
    )


def assemble_folded(tiles, row_count, col_count, own_count, picks):
    span = col_count * own_count
    shaped = tiles.reshape(row_count, col_count, span, picks, own_count)
    block_ids = jnp.arange(row_count, dtype=jnp.int32)
    offsets = jnp.arange(picks, dtype=jnp.int32)
    selector = (
        block_ids[None, None, :] == (block_ids[:, None, None] + offsets[None, :, None]) % row_count
    ).astype(jnp.float32)
    upper = jnp.einsum("rcadk,rdq->raqck", shaped, selector, precision=highest)
    upper = upper.reshape(row_count * span, row_count * span)
    return upper + upper.T - jnp.diag(jnp.diag(upper))


def column_of(matrix, col_index, row_count, col_count, per_device):
    shaped = matrix.reshape(row_count, col_count, per_device, matrix.shape[-1])
    picked = lax.dynamic_index_in_dim(shaped, col_index, 1, keepdims=False)
    return picked.reshape(row_count * per_device, matrix.shape[-1])


def pick_blocks(stacked, row_index, row_count, own_count, picks):
    shaped = stacked.reshape((row_count, own_count) + stacked.shape[1:])
    rolled = jnp.roll(shaped, -row_index, axis=0)[:picks]
    return rolled.reshape((picks * own_count,) + stacked.shape[1:])


def place_blocks(picked, row_index, row_count, own_count, picks):
    shaped = picked.reshape((picks, own_count) + picked.shape[1:])
    padding = jnp.zeros((row_count - picks, own_count) + picked.shape[1:], picked.dtype)
    full = jnp.roll(jnp.concatenate([shaped, padding], axis=0), row_index, axis=0)
    return full.reshape((row_count * own_count,) + picked.shape[1:])


def body(support_views, support_pick, target_views, target_pick, support_labels, target_labels):
    row_count = lax.axis_size("row")
    col_count = lax.axis_size("col")
    row_index = lax.axis_index("row")
    col_index = lax.axis_index("col")
    own_count = support_views.shape[0]
    own_targets = target_views.shape[0]
    channels = support_views.shape[2]
    classes = support_labels.shape[1]
    own_support = choose_view(support_views, support_pick)
    own_target = choose_view(target_views, target_pick)
    support_pack = jnp.concatenate([own_support, self_maps(own_support)], axis=1)
    target_pack = jnp.concatenate([own_target, self_maps(own_target)], axis=1)
    row_pack = lax.all_gather(support_pack, "col", axis=0, tiled=True)
    column_pack, target_block = (
        lax.all_gather(support_pack, "row", axis=0, tiled=True),
        lax.all_gather(target_pack, "row", axis=0, tiled=True),
    )
    row_images = row_pack[:, :channels]
    row_maps = row_pack[:, channels:]
    column_images = column_pack[:, :channels]
    column_maps = column_pack[:, channels:]
    target_images = target_block[:, :channels]
    target_maps = target_block[:, channels:]
    row_start = row_index * col_count * own_count
    row_span = col_count * own_count
    half_count = row_count // 2
    picks = half_count + 1
    chosen_images = pick_blocks(column_images, row_index, row_count, own_count, picks)
    chosen_maps = pick_blocks(column_maps, row_index, row_count, own_count, picks)
    slot_ids = jnp.arange(picks * own_count, dtype=jnp.int32)
    offset_ids = slot_ids // own_count
    inner_ids = slot_ids % own_count
    local_cols = col_index * own_count + inner_ids
    chosen_global = (
        (row_index + offset_ids) % row_count * col_count + col_index
    ) * own_count + inner_ids
    row_ids = jnp.arange(row_span, dtype=jnp.int32)
    keep = jnp.where(
        offset_ids[None, :] == 0,
        row_ids[:, None] <= local_cols[None, :],
        jnp.where(offset_ids[None, :] == half_count, row_index < half_count, True),
    )
    keep_mask = keep.astype(jnp.float32)
    equal_mask = ((offset_ids[None, :] == 0) & (row_ids[:, None] == local_cols[None, :])).astype(
        jnp.float32
    )
    support_tile = blocked_kernel(row_images, row_maps, chosen_images, chosen_maps) * keep_mask
    cross_tile = blocked_kernel(row_images, row_maps, target_images, target_maps)
    onehot_all = (target_labels[:, None] == jnp.arange(classes, dtype=jnp.int32)[None, :]).astype(
        jnp.float32
    ) - 1.0 / classes
    identity = jnp.eye(SUPPORT, dtype=jnp.float32)
    tiles, all_labels = (
        lax.all_gather(support_tile, ("row", "col"), axis=0, tiled=True),
        lax.all_gather(support_labels, ("row", "col"), axis=0, tiled=True),
    )
    support_kernel = assemble_folded(tiles, row_count, col_count, own_count, picks)
    trace_mean = jnp.trace(support_kernel) / SUPPORT
    factor = jnp.linalg.cholesky(support_kernel + ridge_scale * trace_mean * identity)
    alpha = solve_with(factor, all_labels)
    alpha_rows = lax.dynamic_slice_in_dim(alpha, row_start, row_span, 0)
    labels_here = column_of(onehot_all, col_index, row_count, col_count, own_targets)
    predicted = lax.psum(jnp.dot(cross_tile.T, alpha_rows, precision=highest), "row")
    error = predicted - labels_here
    adjoint_part, loss_sum = lax.psum(
        (jnp.dot(cross_tile, error, precision=highest), jnp.sum(error * error)), "col"
    )
    adjoint = lax.all_gather(adjoint_part, "row", axis=0, tiled=True)
    gamma = solve_with(factor, adjoint)
    intersection = jnp.sum(gamma * alpha)
    gamma_rows = lax.dynamic_slice_in_dim(gamma, row_start, row_span, 0)
    cross_weights = jnp.dot(alpha_rows, error.T, precision=highest)
    alpha_chosen = alpha[chosen_global]
    gamma_chosen = gamma[chosen_global]
    folded = -(
        jnp.dot(gamma_rows, alpha_chosen.T, precision=highest)
        + jnp.dot(alpha_rows, gamma_chosen.T, precision=highest)
    )
    support_weights = (
        folded - equal_mask * (0.5 * folded + ridge_scale * intersection / SUPPORT)
    ) * keep_mask
    row_grad, row_map_grad, chosen_grad, chosen_map_grad = blocked_backward(
        row_images, row_maps, chosen_images, chosen_maps, support_weights, True
    )
    col_grad = place_blocks(chosen_grad, row_index, row_count, own_count, picks)
    col_map_grad = place_blocks(chosen_map_grad, row_index, row_count, own_count, picks)
    cross_grad, cross_map_grad, _, _ = blocked_backward(
        row_images, row_maps, target_images, target_maps, cross_weights, False
    )
    row_grad = row_grad + cross_grad
    row_map_grad = row_map_grad + cross_map_grad
    row_send = jnp.concatenate([row_grad, row_map_grad], axis=1)
    col_send = jnp.concatenate([col_grad, col_map_grad], axis=1)
    row_whole = lax.psum(row_send, "col")
    col_whole = lax.psum(col_send, "row")
    row_back = lax.dynamic_slice_in_dim(row_whole, col_index * own_count, own_count, 0)
    col_back = lax.dynamic_slice_in_dim(col_whole, row_index * own_count, own_count, 0)
    combined = row_back + col_back
    support_grad = combined[:, :channels] + self_back(own_support, combined[:, channels:])
    own_start = (row_index * col_count + col_index) * own_count
    label_grad = lax.dynamic_slice_in_dim(gamma, own_start, own_count, 0)
    return (support_grad, label_grad, 0.5 * loss_sum)


def solution(mesh):
    return jax.shard_map(
        body,
        mesh=mesh,
        in_specs=(
            P(("row", "col"), None, None, None),
            P(("row", "col")),
            P(("row", "col"), None, None, None),
            P(("row", "col")),
            P(("row", "col"), None),
            P(),
        ),
        out_specs=(P(("row", "col"), None, None), P(("row", "col"), None), P()),
        check_vma=False,
    )
```

profile of v0, /device:TPU:0, one launch (start us, length us, event | category | flops | bytes accessed | tf_op | source)
XLA Modules:
  0.0 1061.8 jit_solution(16985162748943276678)
XLA Ops:
  13.4 10.3 all_gather.19
  24.6 69.7 %all_gather.22 = f32[256,10]{1,0:T(8,128)S(1)} all-gather(f32[8,10]{1,0:T(8,128)S(1)} %copy-done.22), channel_id=1, replica_groups=mesh['row'=4,'col'=8] {'row','col'}, dimensions={0}, use_global_device_ids=true | all-gather | bytes 10560 | tf_op jit(solution)/shard_map/all_gather | solution.py:265
  94.9 7.8 all_gather.21
  107.6 80.1 %while.70 = (s32[]{:T(128)}, f32[6,64,4]{1,2,0:T(4,128)S(1)}, f32[64,3,1024]{2,0,1:T(8,128)S(1)}, f32[6,4,3,1024]{3,1,2,0:T(4,128)S(1)}, f32[64,3,1024]{2,0,1:T(...) while((s32[]{:T(128)}, f32[6,64,4]{1,2,0:T(4,128)S(1)}, f32[64,3,1024]{2,0,1:T(8,128)S(1)}, ...), condition=%wide.region_4.6_spmd, body=%wide.region_2.5_spmd.sunk | while | flops 19931136 | bytes 54733908 | solution.py:127
  117.9 3.1 multiply_reduce_fusion.27
  131.2 3.1 multiply_reduce_fusion.27
  140.2 3.0 multiply_multiply_fusion.26
  144.4 3.1 multiply_reduce_fusion.27
  157.7 3.1 multiply_reduce_fusion.27
  170.9 3.1 multiply_reduce_fusion.27
  184.2 3.1 multiply_reduce_fusion.27
  187.8 65.5 %all-gather = f32[32,64,24]{1,2,0:T(8,128)S(1)} all-gather(f32[1,64,24]{1,2,0:T(8,128)S(1)} %select_bitcast_fusion.1), channel_id=1, replica_groups=mesh['row'=4,'col'=8] {'row','col'}, dimensions={0}, use_global_device_ids=true | all-gather | bytes 202752 | tf_op jit(solution)/shard_map/all_gather | solution.py:264
  258.8 11.7 %cholesky.49 = f32[128,128]{1,0:T(8,128)S(1)} custom-call(f32[128,128]{1,0:T(8,128)S(1)} %cholesky.115), custom_call_target="Cholesky" | custom-call | tf_op jit(solution)/shard_map/jit(cholesky)/cholesky | solution.py:269
  270.6 9.8 custom-call.17
  280.9 11.7 %cholesky.103 = f32[128,128]{1,0:T(8,128)S(1)} custom-call(f32[128,128]{1,0:T(8,128)S(1)} %convolution_subtract_fusion), custom_call_target="Cholesky" | custom-call | tf_op jit(solution)/shard_map/jit(cholesky)/cholesky | solution.py:269
  295.7 4.3 while.74
  300.6 20.5 %custom-call.29 = f32[2,128,128]{1,2,0:T(8,128)S(1)} custom-call(f32[2,128,128]{2,1,0:T(8,128)} %copy-done.27), custom_call_target="InvertDiagBlocksLowerTriangular" | custom-call | tf_op jit(solution)/shard_map/triangular_solve/custom-call.4 | solution.py:173
  323.0 117.2 %while.71 = (s32[]{:T(128)}, f32[8,64,4]{1,2,0:T(4,128)}, f32[64,3,1024]{2,0,1:T(8,128)S(1)}, f32[8,4,3,1024]{3,1,2,0:T(4,128)}, f32[64,3,1024]{2,0,1:T(8,128)S(1)}, /*index=5*/f32[8,4,3,1024]{3,1,2,0:T(4,128)}, s32[]{:T(128)}) while((s32[]{:T(128)}, f32[8,64,4]{1,2,0:T(4,128)}, f32[64,3,1024]{2,0,1:T(8,128)S(1)}, ...), condition=%wide.region_14.16_spmd, body=%wide.region_12.15_spmd.sunk | while | flops 19931136 | bytes 54733392 | solution.py:127
  334.1 3.1 multiply_reduce_fusion.28
  348.7 3.1 multiply_reduce_fusion.28
  363.4 3.1 multiply_reduce_fusion.28
  378.0 3.1 multiply_reduce_fusion.28
  392.6 3.1 multiply_reduce_fusion.28
  407.2 3.1 multiply_reduce_fusion.28
  421.8 3.1 multiply_reduce_fusion.28
  436.5 3.1 multiply_reduce_fusion.28
  443.1 6.6 psum.35
  454.0 20.6 %all-reduce.111 = (f32[64,10]{0,1:T(8,128)S(1)}, f32[]{:T(128)}) all-reduce(f32[64,10]{0,1:T(8,128)} %fusion.91, f32[]{:T(128)} %multiply_reduce_fusion.19), channel_id=1, replica_groups=mesh['row'=4,'col'=8] {'col'}, use_global_device_ids=true, to_apply=%region_16.20 | all-reduce | flops 641 | bytes 5128 | tf_op jit(solution)/shard_map/psum | solution.py:275
  474.6 5.2 all-gather.1
  489.0 222.6 %while.72 = (s32[]{:T(128)}, f32[64,3,1024]{2,0,1:T(8,128)S(1)}, f32[64,3,1024]{2,0,1:T(8,128)S(1)}, f32[6,4,3,1024]{3,1,0,2:T(4,128)}, f32[6,4,3,1024]{3,1,0,2:...) while((s32[]{:T(128)}, f32[64,3,1024]{2,0,1:T(8,128)S(1)}, ...), condition=%wide.region_31.35_spmd.clone, body=%wide.region_18.34_spmd.clone.sunk | while | flops 38808064 | bytes 129204872 | solution.py:152
  719.3 243.5 %while.73 = (s32[]{:T(128)}, f32[64,3,1024]{2,0,1:T(8,128)S(1)}, f32[64,3,1024]{2,0,1:T(8,128)S(1)}, f32[64,3,1024]{2,0,1:T(8,128)S(1)}, f32[8,4,3,1024]{3,1,2,0...) while((s32[]{:T(128)}, f32[64,3,1024]{2,0,1:T(8,128)S(1)}, ...), condition=%wide.region_39.43_spmd.clone, body=%wide.region_32.42_spmd.clone.sunk | while | flops 36203008 | bytes 120111224 | solution.py:152
  967.8 83.4 %all-reduce.115.cloned.1.call-done = f32[64,6,1024]{2,0,1:T(8,128)} async-done(((f32[64,6,1024]{2,0,1:T(8,128)}), f32[64,6,1024]{2,0,1:T(8,128)}) %all-reduce.115.cloned.1.call-update) | async-done | bytes 1572880 | tf_op jit(solution)/shard_map/psum | solution.py:304
  (1042 shorter events, 632.2 us)
Async XLA Ops:
  7.2 3.4 copy-start.11
  7.2 99.0 %all-gather.4.cloned.1.call-start = ((), (), s32[]{:S(2)}) async-start(), calls=%async_computation | async-start | bytes 1769472 | tf_op jit(solution)/shard_map/all_gather | solution.py:223
  7.2 4.8 copy-start.17
  7.2 4.8 copy-start.19
  10.9 1.6 copy-start.9
  13.4 954.4 %all-reduce.117.cloned.1.call-start = ((), (), s32[]{:S(2)}) async-start(), calls=%async_computation.2 | async-start | bytes 1572864 | tf_op jit(solution)/shard_map/psum | solution.py:305
  23.9 0.7 copy-start.22
  102.8 1.8 copy-start.23
  105.5 82.2 %copy-start.24 = (s32[24]{0:T(128)}, s32[24]{0:T(128)S(1)}, u32[]{:S(2)}) copy-start(s32[24]{0:T(128)S(1)} %fusion.81) | copy-start | bytes 292
  105.5 82.2 %copy-start.25 = (pred[24]{0:T(512)(128)(4,1)}, pred[24]{0:T(512)(128)(4,1)S(1)}, u32[]{:S(2)}) copy-start(pred[24]{0:T(512)(128)(4,1)S(1)} %get-tuple-element.1339) | copy-start | bytes 76
  105.5 82.2 %copy-start.26 = (pred[24]{0:T(512)(128)(4,1)}, pred[24]{0:T(512)(128)(4,1)S(1)}, u32[]{:S(2)}) copy-start(pred[24]{0:T(512)(128)(4,1)S(1)} %get-tuple-element.1340) | copy-start | bytes 76
  187.7 66.6 %copy-start.7 = (f32[6,4,3,1024]{3,1,2,0:T(4,128)}, f32[6,4,3,1024]{3,1,2,0:T(4,128)S(1)}, u32[]{:S(2)}) copy-start(f32[6,4,3,1024]{3,1,2,0:T(4,128)S(1)} %get-tuple-element.2067) | copy-start | bytes 884740
  187.7 66.9 %copy-start.8 = (f32[6,4,3,1024]{3,1,2,0:T(4,128)}, f32[6,4,3,1024]{3,1,2,0:T(4,128)S(1)}, u32[]{:S(2)}) copy-start(f32[6,4,3,1024]{3,1,2,0:T(4,128)S(1)} %get-tuple-element.2068) | copy-start | bytes 884740
  300.0 0.6 copy-start.27
  323.0 126.7 %copy-start.16 = (f32[32,10]{0,1:T(8,128)S(1)}, f32[32,10]{0,1:T(8,128)}, u32[]{:S(2)}) copy-start(f32[32,10]{0,1:T(8,128)} %reshape.516) | copy-start | bytes 3844
  440.2 48.8 %copy-start.2 = (f32[64,3,1024]{2,0,1:T(8,128)S(1)}, f32[64,3,1024]{2,0,1:T(8,128)}, u32[]{:S(2)}) copy-start(f32[64,3,1024]{2,0,1:T(8,128)} %custom-call.22) | copy-start | bytes 2359300
  440.2 48.8 %copy-start.4 = (f32[64,3,1024]{2,0,1:T(8,128)S(1)}, f32[64,3,1024]{2,0,1:T(8,128)}, u32[]{:S(2)}) copy-start(f32[64,3,1024]{2,0,1:T(8,128)} %custom-call.23) | copy-start | bytes 2359300
  441.1 0.6 copy-start.21
  483.9 5.1 copy-start.12
  484.3 4.7 copy-start.14
  711.7 5.8 copy-start.3
  711.7 5.8 copy-start.5
  717.6 1.2 copy-start
  717.6 1.6 copy-start.1
  718.7 332.5 %all-reduce.115.cloned.1.call-start = ((), (), s32[]{:S(2)}) async-start(), calls=%async_computation.1 | async-start | bytes 3145728 | tf_op jit(solution)/shard_map/psum | solution.py:304
  962.8 1.4 copy-start.6
  965.6 0.7 copy-start.13
  965.6 0.7 copy-start.15
  965.6 86.7 %copy-start.18 = (pred[1024]{0:T(1024)(128)(4,1)S(1)}, pred[1024]{0:T(1024)(128)(4,1)}, u32[]{:S(2)}) copy-start(pred[1024]{0:T(1024)(128)(4,1)} %copy-done.17) | copy-start | bytes 3076
  965.6 86.7 %copy-start.20 = (pred[1024]{0:T(1024)(128)(4,1)S(1)}, pred[1024]{0:T(1024)(128)(4,1)}, u32[]{:S(2)}) copy-start(pred[1024]{0:T(1024)(128)(4,1)} %copy-done.19) | copy-start | bytes 3076
  965.6 87.6 %copy-start.10 = (f32[8,3,1024]{2,1,0:T(4,128)S(1)}, f32[8,3,1024]{2,1,0:T(4,128)}, u32[]{:S(2)}) copy-start(f32[8,3,1024]{2,1,0:T(4,128)} %copy-done.9) | copy-start | bytes 294916
Sparse Core Ops, SparseCore 0:
  13.5 47.3 all-gather.3
  718.8 31.1 all-reduce.116
  965.7 85.3 all-reduce.114
where the time goes:
time: 1070 us; the launch traced here: 1060 us
  other arithmetic  564 us (53%)
  blocking collectives  186 us (17%)
  local copies, waits for them, and re-layouts  158 us (15%)
  waiting for transfers between devices  83.5 us (8%)
  loops' own time  41.1 us (4%)
  between operations  19.1 us (2%)
  matrix products  11 us (1%)
    div x56, other arithmetic, arc(): value = scale_map * (sine + (jnp.pi - angle) * cosine) / jnp.pi  165 us
    psum x1, waiting for transfers between devices, body(): row_whole = lax.psum(row_send, 'col')  83.4 us
    add x133, other arithmetic, average(): across = surface + leftward + rightward  83.2 us
    all_gather x1, blocking collectives, body(): lax.all_gather(support_labels, ('row', 'col'), axis=0, tiled=True)  69.7 us
    all_gather x1, blocking collectives, body(): lax.all_gather(support_tile, ('row', 'col'), axis=0, tiled=True)  65.5 us
    mul x40, other arithmetic, pair_backward(): grad = average(grad * slopes[layer])  56.8 us
    reduce_sum x24, other arithmetic, pair_backward(): first_parts.insert(0, jnp.sum(scaled, axis=1) / first_maps[:, layer])  53.7 us
    slice x135, local copies, waits for them, and re-layouts, shifted(): return jnp.concatenate([padding, surface[..., :extent + offset]], axis=-1)  49 us
  transfers between devices with their start and end apart: 3, of which 1 were waited for; matrix products, arithmetic and copies ran while one was open for 24% of the time, Pallas kernels for 0%

commit v1 on v0

--- a/solution.py
+++ b/solution.py
@@ -301,7 +301,7 @@
     row_map_grad = row_map_grad + cross_map_grad
     row_send = jnp.concatenate([row_grad, row_map_grad], axis=1)
     col_send = jnp.concatenate([col_grad, col_map_grad], axis=1)
-    row_whole = lax.psum(row_send, "col")
+    row_whole = jnp.sum(lax.all_gather(row_send, "col"), axis=0)
     col_whole = lax.psum(col_send, "row")
     row_back = lax.dynamic_slice_in_dim(row_whole, col_index * own_count, own_count, 0)
     col_back = lax.dynamic_slice_in_dim(col_whole, row_index * own_count, own_count, 0)

time: 1070 us -> 1140 us (1.065)
  waiting for transfers between devices: 83.5 us -> 200 us
  other arithmetic: 564 us -> 525 us
  loops' own time: 41.1 us -> 23.7 us
  local copies, waits for them, and re-layouts: 158 us -> 173 us
    all_gather x0 -> x1, waiting for transfers between devices: none -> 169 us  [body(): row_whole = jnp.sum(lax.all_gather(row_send, 'col'), axis=0)]
    psum x1 -> x0, waiting for transfers between devices: 83.4 us -> none  [body(): row_whole = lax.psum(row_send, 'col')]
    psum x1, waiting for transfers between devices: 0.02 us -> 30.6 us  [body(): col_whole = lax.psum(col_send, 'row')]
    another operation x2, loops' own time: 38.8 us -> 21.2 us  [blocked_backward(): lax.scan(one_block, start, (second.reshape((block_count, block_width) + s...]
    add x14, other arithmetic: 24.2 us -> 6.79 us  [one_block(): carry[0] + grad_first]
    while x0 -> x88, local copies, waits for them, and re-layouts: none -> 16.9 us
  transfers between devices with their start and end apart: 3 -> 3, of which waited for: 1 -> 2; matrix products, arithmetic and copies ran while one was open for 24% -> 1% of each run, Pallas kernels for 0% -> 0%
where the time goes in v1:
time: 1140 us; the launch traced here: 1130 us
  other arithmetic  525 us (46%)
  waiting for transfers between devices  200 us (18%)
  blocking collectives  184 us (16%)
  local copies, waits for them, and re-layouts  173 us (15%)
  loops' own time  23.7 us (2%)
  between operations  19.3 us (2%)
    all_gather x1, waiting for transfers between devices, body(): row_whole = jnp.sum(lax.all_gather(row_send, 'col'), axis=0)  169 us
    div x56, other arithmetic, arc(): value = scale_map * (sine + (jnp.pi - angle) * cosine) / jnp.pi  165 us
    add x133, other arithmetic, average(): across = surface + leftward + rightward  83.4 us
    all_gather x1, blocking collectives, body(): lax.all_gather(support_labels, ('row', 'col'), axis=0, tiled=True)  71.3 us
    all_gather x1, blocking collectives, body(): lax.all_gather(support_tile, ('row', 'col'), axis=0, tiled=True)  65.6 us
    mul x40, other arithmetic, pair_backward(): grad = average(grad * slopes[layer])  57 us
    reduce_sum x24, other arithmetic, pair_backward(): first_parts.insert(0, jnp.sum(scaled, axis=1) / first_maps[:, layer])  53.7 us
    slice x135, local copies, waits for them, and re-layouts, shifted(): return jnp.concatenate([surface[..., offset:], padding], axis=-1)  49.1 us
  transfers between devices with their start and end apart: 3, of which 2 were waited for; matrix products, arithmetic and copies ran while one was open for 1% of the time, Pallas kernels for 0%

profile of v1, /device:TPU:0, one launch (start us, length us, event | category | flops | bytes accessed | tf_op | source)
XLA Modules:
  0.0 1131.6 jit_solution(16989059242025566253)
XLA Ops:
  15.9 71.3 %all_gather.28 = f32[256,10]{1,0:T(8,128)S(1)} all-gather(f32[8,10]{1,0:T(8,128)S(1)} %copy-done.30), channel_id=1, replica_groups=mesh['row'=4,'col'=8] {'row','col'}, dimensions={0}, use_global_device_ids=true | all-gather | bytes 10560 | tf_op jit(solution)/shard_map/all_gather | solution.py:265
  88.5 7.5 all_gather.27
  97.8 8.8 all_gather.25
  110.6 85.1 %while.70 = (s32[]{:T(128)}, f32[6,64,4]{1,2,0:T(4,128)S(1)}, f32[64,3,1024]{2,0,1:T(8,128)S(1)}, f32[6,4,3,1024]{3,1,2,0:T(4,128)S(1)}, f32[64,3,1024]{2,0,1:T(...) while((s32[]{:T(128)}, f32[6,64,4]{1,2,0:T(4,128)S(1)}, f32[64,3,1024]{2,0,1:T(8,128)S(1)}, ...), condition=%wide.region_4.6_spmd, body=%wide.region_2.5_spmd.sunk | while | flops 19931136 | bytes 54733916 | solution.py:127
  121.7 3.1 multiply_reduce_fusion.27
  135.8 3.1 multiply_reduce_fusion.27
  149.9 3.1 multiply_reduce_fusion.27
  164.0 3.1 multiply_reduce_fusion.27
  178.0 3.1 multiply_reduce_fusion.27
  192.1 3.1 multiply_reduce_fusion.27
  195.8 65.6 %all-gather.1 = f32[32,64,24]{1,2,0:T(8,128)S(1)} all-gather(f32[1,64,24]{1,2,0:T(8,128)S(1)} %select_bitcast_fusion.1), channel_id=1, replica_groups=mesh['row'=4,'col'=8] {'row','col'}, dimensions={0}, use_global_device_ids=true | all-gather | bytes 202752 | tf_op jit(solution)/shard_map/all_gather | solution.py:264
  266.8 11.7 %cholesky.49 = f32[128,128]{1,0:T(8,128)S(1)} custom-call(f32[128,128]{1,0:T(8,128)S(1)} %cholesky.115), custom_call_target="Cholesky" | custom-call | tf_op jit(solution)/shard_map/jit(cholesky)/cholesky | solution.py:269
  279.8 9.8 custom-call.17
  290.8 11.7 %cholesky.103 = f32[128,128]{1,0:T(8,128)S(1)} custom-call(f32[128,128]{1,0:T(8,128)S(1)} %convolution_subtract_fusion), custom_call_target="Cholesky" | custom-call | tf_op jit(solution)/shard_map/jit(cholesky)/cholesky | solution.py:269
  303.3 112.7 %while.71 = (s32[]{:T(128)}, f32[8,64,4]{1,2,0:T(4,128)S(1)}, f32[64,3,1024]{2,0,1:T(8,128)S(1)}, f32[8,4,3,1024]{3,1,2,0:T(4,128)}, f32[64,3,1024]{2,0,1:T(8,12...) while((s32[]{:T(128)}, f32[8,64,4]{1,2,0:T(4,128)S(1)}, f32[64,3,1024]{2,0,1:T(8,128)S(1)}, ...), condition=%wide.region_14.16_spmd, body=%wide.region_12.15_spmd.sunk | while | flops 19931136 | bytes 54733916 | solution.py:127
  328.4 3.1 multiply_reduce_fusion.28
  342.4 3.1 multiply_reduce_fusion.28
  356.4 3.1 multiply_reduce_fusion.28
  370.4 3.1 multiply_reduce_fusion.28
  384.5 3.1 multiply_reduce_fusion.28
  398.5 3.1 multiply_reduce_fusion.28
  412.5 3.1 multiply_reduce_fusion.28
  421.3 5.5 while.74
  426.9 20.5 %custom-call.29 = f32[2,128,128]{1,2,0:T(8,128)S(1)} custom-call(f32[2,128,128]{2,1,0:T(8,128)} %get-tuple-element.627), custom_call_target="InvertDiagBlocksLowerTriangular" | custom-call | tf_op jit(solution)/shard_map/triangular_solve/custom-call.4 | solution.py:173
  448.8 5.8 psum.28
  456.3 20.5 %all-reduce.111 = (f32[64,10]{0,1:T(8,128)S(1)}, f32[]{:T(128)}) all-reduce(f32[64,10]{0,1:T(8,128)S(1)} %fusion.88, f32[]{:T(128)} %multiply_reduce_fusion.19), channel_id=1, replica_groups=mesh['row'=4,'col'=8] {'col'}, use_global_device_ids=true, to_apply=%region_16.20 | all-reduce | flops 641 | bytes 5128 | tf_op jit(solution)/shard_map/psum | solution.py:275
  476.7 5.2 all-gather.2
  487.5 231.2 %while.73 = (s32[]{:T(128)}, f32[64,3,1024]{2,0,1:T(8,128)}, f32[64,3,1024]{2,0,1:T(8,128)}, f32[64,3,1024]{2,0,1:T(8,128)S(1)}, f32[8,4,3,1024]{3,1,2,0:T(4,128...) while((s32[]{:T(128)}, f32[64,3,1024]{2,0,1:T(8,128)}, ...), condition=%wide.region_39.43_spmd.clone, body=%wide.region_32.42_spmd.clone.sunk | while | flops 36203008 | bytes 132694256 | solution.py:152
  719.7 187.5 %while.72 = (s32[]{:T(128)}, f32[64,3,1024]{2,0,1:T(8,128)S(1)}, f32[64,3,1024]{2,0,1:T(8,128)S(1)}, f32[6,4,3,1024]{3,1,0,2:T(4,128)}, f32[6,4,3,1024]{3,1,0,2:...) while((s32[]{:T(128)}, f32[64,3,1024]{2,0,1:T(8,128)S(1)}, ...), condition=%wide.region_31.35_spmd.clone, body=%wide.region_18.34_spmd.clone.sunk | while | flops 38808064 | bytes 129253584 | solution.py:152
  914.7 169.1 %all-gather.8.cloned.1.call-done = f32[512,6,1024]{2,0,1:T(8,128)} async-done(((f32[64,6,1024]{2,0,1:T(8,128)}), f32[512,6,1024]{2,0,1:T(8,128)}) %all-gather.8.cloned.1.call-update) | async-done | bytes 12582928 | tf_op jit(solution)/shard_map/all_gather | solution.py:304
  1083.9 6.2 reduce_sum.391
  1090.1 30.6 %all-reduce.114.cloned.1.call-done = f32[32,6,1024]{2,1,0:T(8,128)} async-done(((f32[32,6,1024]{2,1,0:T(8,128)}), f32[32,6,1024]{2,1,0:T(8,128)}) %all-reduce.114.cloned.1.call-update) | async-done | bytes 786448 | tf_op jit(solution)/shard_map/psum | solution.py:305
  (1146 shorter events, 604.0 us)
Async XLA Ops:
  7.2 101.9 %all-gather.6.cloned.1.call-start = ((), (), s32[]{:S(2)}) async-start(), calls=%async_computation | async-start | bytes 1769472 | tf_op jit(solution)/shard_map/all_gather | solution.py:223
  7.2 5.9 copy-start.21
  7.2 5.9 copy-start.23
  10.0 3.3 copy-start.8
  12.3 2.1 copy-start.31
  13.2 2.7 copy-start.30
  14.3 1069.5 %all-gather.8.cloned.1.call-start = ((), (), s32[]{:S(2)}) async-start(), calls=%async_computation.2 | async-start | bytes 14155776 | tf_op jit(solution)/shard_map/all_gather | solution.py:304
  96.0 1.8 copy-start.11
  108.4 87.3 %copy-start.33 = (s32[24]{0:T(128)}, s32[24]{0:T(128)S(1)}, u32[]{:S(2)}) copy-start(s32[24]{0:T(128)S(1)} %fusion.78) | copy-start | bytes 292
  108.4 87.3 %copy-start.35 = (pred[24]{0:T(512)(128)(4,1)}, pred[24]{0:T(512)(128)(4,1)S(1)}, u32[]{:S(2)}) copy-start(pred[24]{0:T(512)(128)(4,1)S(1)} %get-tuple-element.1293) | copy-start | bytes 76
  108.4 87.3 %copy-start.37 = (pred[24]{0:T(512)(128)(4,1)}, pred[24]{0:T(512)(128)(4,1)S(1)}, u32[]{:S(2)}) copy-start(pred[24]{0:T(512)(128)(4,1)S(1)} %get-tuple-element.1294) | copy-start | bytes 76
  195.7 67.1 %copy-start.7 = (f32[6,4,3,1024]{3,1,2,0:T(4,128)}, f32[6,4,3,1024]{3,1,2,0:T(4,128)S(1)}, u32[]{:S(2)}) copy-start(f32[6,4,3,1024]{3,1,2,0:T(4,128)S(1)} %get-tuple-element.2022) | copy-start | bytes 884740
  266.5 36.7 %copy-start.10 = (f32[8,4,3,1024]{3,1,2,0:T(4,128)S(1)}, f32[8,4,3,1024]{3,1,2,0:T(4,128)}, u32[]{:S(2)}) copy-start(f32[8,4,3,1024]{3,1,2,0:T(4,128)} %copy.279) | copy-start | bytes 1179652
  303.3 112.8 %copy-start.32 = (f32[128]{0:T(128)S(1)}, f32[128]{0:T(128)}, u32[]{:S(2)}) copy-start(f32[128]{0:T(128)} %get-tuple-element.1246) | copy-start | bytes 1540
  303.3 118.0 %copy-start.38 = (s32[2]{0:T(128)S(1)}, s32[2]{0:T(128)}, u32[]{:S(2)}) copy-start(s32[2]{0:T(128)} %iota_multiply_fusion) | copy-start | bytes 28
  418.6 28.8 %copy-start.13 = (f32[256,10]{1,0:T(8,128)S(1)}, f32[256,10]{1,0:T(8,128)}, u32[]{:S(2)}) copy-start(f32[256,10]{1,0:T(8,128)} %copy-done.12) | copy-start | bytes 30724
  419.5 28.1 %copy-start.27 = (f32[128,10]{0,1:T(8,128)S(1)}, f32[128,10]{0,1:T(8,128)}, u32[]{:S(2)}) copy-start(f32[128,10]{0,1:T(8,128)} %copy.308) | copy-start | bytes 15364
  421.2 33.4 %copy-start.20 = (f32[32,10]{0,1:T(8,128)S(1)}, f32[32,10]{0,1:T(8,128)}, u32[]{:S(2)}) copy-start(f32[32,10]{0,1:T(8,128)} %reshape.516) | copy-start | bytes 3844
  448.7 28.0 %copy-start.25 = (f32[64,10]{0,1:T(8,128)}, f32[64,10]{0,1:T(8,128)S(1)}, u32[]{:S(2)}) copy-start(f32[64,10]{0,1:T(8,128)S(1)} %fusion.59) | copy-start | bytes 7684
  482.7 4.8 copy-start.16
  483.1 4.3 copy-start.18
  487.5 231.3 %copy-start.26 = (f32[64,10]{0,1:T(8,128)S(1)}, f32[64,10]{0,1:T(8,128)}, u32[]{:S(2)}) copy-start(f32[64,10]{0,1:T(8,128)} %copy-done.25) | copy-start | bytes 7684
  487.5 231.3 %copy-start.34 = (s32[24]{0:T(128)S(1)}, s32[24]{0:T(128)}, u32[]{:S(2)}) copy-start(s32[24]{0:T(128)} %copy-done.33) | copy-start | bytes 292
  487.5 231.3 %copy-start.36 = (pred[24]{0:T(512)(128)(4,1)S(1)}, pred[24]{0:T(512)(128)(4,1)}, u32[]{:S(2)}) copy-start(pred[24]{0:T(512)(128)(4,1)} %copy-done.35) | copy-start | bytes 76
  487.5 232.2 %copy-start = (f32[64,3,1024]{2,0,1:T(8,128)S(1)}, f32[64,3,1024]{2,0,1:T(8,128)}, u32[]{:S(2)}) copy-start(f32[64,3,1024]{2,0,1:T(8,128)} %custom-call.23) | copy-start | bytes 2359300
  487.5 232.2 %copy-start.1 = (f32[64,3,1024]{2,0,1:T(8,128)S(1)}, f32[64,3,1024]{2,0,1:T(8,128)}, u32[]{:S(2)}) copy-start(f32[64,3,1024]{2,0,1:T(8,128)} %custom-call.22) | copy-start | bytes 2359300
  737.4 1.7 copy-start.28
  765.7 1.7 copy-start.28
  910.0 210.7 %all-reduce.114.cloned.1.call-start = ((), (), s32[]{:S(2)}) async-start(), calls=%async_computation.1 | async-start | bytes 2097152 | tf_op jit(solution)/shard_map/psum | solution.py:305
  1083.9 38.1 %copy-start.22 = (pred[1024]{0:T(1024)(128)(4,1)S(1)}, pred[1024]{0:T(1024)(128)(4,1)}, u32[]{:S(2)}) copy-start(pred[1024]{0:T(1024)(128)(4,1)} %copy-done.21) | copy-start | bytes 3076
  1083.9 38.1 %copy-start.24 = (pred[1024]{0:T(1024)(128)(4,1)S(1)}, pred[1024]{0:T(1024)(128)(4,1)}, u32[]{:S(2)}) copy-start(pred[1024]{0:T(1024)(128)(4,1)} %copy-done.23) | copy-start | bytes 3076
  1090.1 32.8 %copy-start.9 = (f32[8,3,1024]{2,1,0:T(4,128)S(1)}, f32[8,3,1024]{2,1,0:T(4,128)}, u32[]{:S(2)}) copy-start(f32[8,3,1024]{2,1,0:T(4,128)} %copy-done.8) | copy-start | bytes 294916
  (48 other events, 57.1 us)
Sparse Core Ops, SparseCore 0:
  14.5 47.3 all-gather.5
  910.2 173.6 all-gather.7
  1086.2 34.4 all-reduce.113
